TPU v7x, 32 devices: a whole 2x2x4 slice. The times are simulated.
32 devices in a mesh: expert: 4 (over y, x), dp: 8 (over z, core).
Axes of the slice: x: 2, y: 2, z: 4, core: 2. Of those that a mesh axis runs over, the one named last changes fastest.
Arguments:
- tokens: bfloat16 [1024, 5120], P('dp', 'expert'), may hold values from -6 to 6
- routes: int32 [1024, 2], P('dp'), may hold values from 0 to 7, all different within a row; in each aligned block of 128 rows (0 to 127, 128 to 255, ...) at most 48 rows name the same one
- combine: bfloat16 [1024, 2], P('dp'), may hold values from 0.099609375 to 1
- cotangent: bfloat16 [1024, 5120], P('dp', 'expert'), may hold values from -1.5 to 1.5
- w_gate: bfloat16 [8, 5120, 768], P('dp', 'expert'), may hold values from -0.078125 to 0.078125
- w_up: bfloat16 [8, 5120, 768], P('dp', 'expert'), may hold values from -0.078125 to 0.078125
- w_down: bfloat16 [8, 768, 5120], P('dp', None, 'expert'), may hold values from -0.21875 to 0.21875
Outputs:
- token_grad: bfloat16 [1024, 5120], P('dp', 'expert')
- combine_grad: float32 [1024, 2], P('dp')
- grad_gate: bfloat16 [8, 5120, 768], P('dp', 'expert')
- grad_up: bfloat16 [8, 5120, 768], P('dp', 'expert')
- grad_down: bfloat16 [8, 768, 5120], P('dp', None, 'expert')
Inputs may be any that keep to these rules, and one draw needn't show every extreme that they name: `routes`: each token names 2 different experts. The tokens of one group name any one expert at most 48 times, a bound that some block reaches.
All inputs are finite; a program needn't handle non-finite values.
Results may differ from a plain program's by a relative error of at most 0.018.
Values may be sent and summed in bfloat16 or wider, within the bound.
No kernel may reach another device: no remote copies, remote signals or barrier semaphores. Data moves between devices by JAX's collectives and lax.ppermute only.
A program may use at most 64 MiB of HBM per device.

v0:
```python
import jax
import jax.numpy as jnp
from jax import lax
from jax.sharding import PartitionSpec as P


def contract_last(matrix_a, matrix_b):
    return lax.dot_general(
        matrix_a, matrix_b, (((1,), (1,)), ((), ())), preferred_element_type=jnp.float32
    )


def contract_first(matrix_a, matrix_b):
    return lax.dot_general(
        matrix_a, matrix_b, (((0,), (0,)), ((), ())), preferred_element_type=jnp.float32
    )


def swiglu_grads(pre_gate, pre_up, back_hidden, weights):
    sigmas = jax.nn.sigmoid(pre_gate)
    active = pre_gate * sigmas
    hidden = (active * pre_up).astype(jnp.bfloat16)
    scaled = weights[:, None] * back_hidden
    grad_gate_pre = (scaled * pre_up * sigmas * (1.0 + pre_gate * (1.0 - sigmas))).astype(
        jnp.bfloat16
    )
    grad_up_pre = (scaled * active).astype(jnp.bfloat16)
    return (hidden, grad_gate_pre, grad_up_pre)


def body(tokens, routes, combine, cotangent, w_gate, w_up, w_down):
    tok_rows, slice_width = tokens.shape
    top_routes = routes.shape[1]
    experts = lax.axis_size("dp")
    capacity = 3 * tok_rows * top_routes // (2 * experts)
    route_count = tok_rows * top_routes
    slot_total = experts * capacity
    route_flat = routes.reshape(route_count)
    onehot = (route_flat[:, None] == jnp.arange(experts, dtype=jnp.int32)[None, :]).astype(
        jnp.int32
    )
    slot_rank = jnp.sum((jnp.cumsum(onehot, axis=0) - onehot) * onehot, axis=1)
    places = route_flat * capacity + slot_rank
    source = jnp.full((slot_total,), route_count, jnp.int32)
    source = source.at[places].set(jnp.arange(route_count, dtype=jnp.int32))
    blank_row = jnp.zeros((1, slice_width), jnp.bfloat16)
    token_send = jnp.concatenate([tokens, blank_row], axis=0)[source // top_routes]
    cot_send = jnp.concatenate([cotangent, blank_row], axis=0)[source // top_routes]
    comb_send = jnp.concatenate(
        [combine.reshape(route_count), jnp.zeros((1,), jnp.bfloat16)], axis=0
    )[source]
    arrived_tok, arrived_cot, arrived_comb = (
        lax.all_to_all(
            token_send.reshape(experts, capacity, slice_width),
            "dp",
            split_axis=0,
            concat_axis=0,
            tiled=True,
        ),
        lax.all_to_all(
            cot_send.reshape(experts, capacity, slice_width),
            "dp",
            split_axis=0,
            concat_axis=0,
            tiled=True,
        ),
        lax.all_to_all(
            comb_send.reshape(experts, capacity), "dp", split_axis=0, concat_axis=0, tiled=True
        ),
    )
    token_slots = arrived_tok.reshape(slot_total, slice_width)
    cot_slots = arrived_cot.reshape(slot_total, slice_width)
    comb_slots = arrived_comb.reshape(slot_total).astype(jnp.float32)
    gate_mat = w_gate[0]
    up_mat = w_up[0]
    down_mat = w_down[0]
    partials = jnp.stack(
        [
            jnp.dot(token_slots, gate_mat, preferred_element_type=jnp.float32),
            jnp.dot(token_slots, up_mat, preferred_element_type=jnp.float32),
            contract_last(cot_slots, down_mat),
        ],
        axis=1,
    )
    summed = lax.psum_scatter(
        partials.astype(jnp.bfloat16), "expert", scatter_dimension=2, tiled=True
    ).astype(jnp.float32)
    hidden_part, gate_part, up_part = swiglu_grads(
        summed[:, 0], summed[:, 1], summed[:, 2], comb_slots
    )
    slot_comb = jnp.sum(hidden_part.astype(jnp.float32) * summed[:, 2], axis=1)
    joined = lax.all_gather(
        jnp.stack([hidden_part, gate_part, up_part], axis=1), "expert", axis=2, tiled=True
    )
    hidden = joined[:, 0]
    grad_gate_pre = joined[:, 1]
    grad_up_pre = joined[:, 2]
    slot_dx = contract_last(grad_gate_pre, gate_mat) + contract_last(grad_up_pre, up_mat)
    scaled_dy = (comb_slots[:, None] * cot_slots.astype(jnp.float32)).astype(jnp.bfloat16)
    grad_gate = contract_first(token_slots, grad_gate_pre).astype(jnp.bfloat16)[None]
    grad_up = contract_first(token_slots, grad_up_pre).astype(jnp.bfloat16)[None]
    grad_down = contract_first(hidden, scaled_dy).astype(jnp.bfloat16)[None]
    back_dx, back_comb = (
        lax.all_to_all(
            slot_dx.reshape(experts, capacity, slice_width).astype(jnp.bfloat16),
            "dp",
            split_axis=0,
            concat_axis=0,
            tiled=True,
        ).astype(jnp.float32),
        lax.all_to_all(
            slot_comb.reshape(experts, capacity).astype(jnp.bfloat16),
            "dp",
            split_axis=0,
            concat_axis=0,
            tiled=True,
        ).astype(jnp.float32),
    )
    route_dx = back_dx.reshape(slot_total, slice_width)[places].reshape(
        tok_rows, top_routes, slice_width
    )
    token_grad = jnp.sum(route_dx, axis=1).astype(jnp.bfloat16)
    comb_part = back_comb.reshape(slot_total)[places].reshape(tok_rows, top_routes)
    combine_grad = lax.psum(comb_part, "expert")
    return (token_grad, combine_grad, grad_gate, grad_up, grad_down)


def solution(mesh):
    in_specs = (
        P("dp", "expert"),
        P("dp", None),
        P("dp", None),
        P("dp", "expert"),
        P("dp", "expert", None),
        P("dp", "expert", None),
        P("dp", None, "expert"),
    )
    out_specs = (
        P("dp", "expert"),
        P("dp", None),
        P("dp", "expert", None),
        P("dp", "expert", None),
        P("dp", None, "expert"),
    )
    return jax.shard_map(body, mesh=mesh, in_specs=in_specs, out_specs=out_specs, check_vma=False)
```

profile of v0, /device:TPU:0, one launch (start us, length us, event | category | flops | bytes accessed | tf_op | source)
XLA Modules:
  0.0 218.3 jit_solution(15409593457587932573)
XLA Ops:
  7.2 0.0 copy-start
  7.2 0.8 broadcast_multiply_fusion
  8.0 0.8 copy.25
  8.8 0.1 eq.29
  8.9 0.1 eq.25
  9.1 0.1 copy.24
  9.2 0.1 mul.76
  9.3 0.6 reduce-window.6
  9.9 0.2 slice_reduce_fusion
  10.2 0.1 fusion.38
  10.3 1.4 scatter_custom_fusion
  11.7 1.0 concatenate.9
  12.7 2.8 %gather_fusion = bf16[384,1280]{1,0:T(8,128)(2,1)} fusion(bf16[129,1280]{1,0:T(8,128)(2,1)S(1)} %concatenate.9, s32[1024]{0:T(1024)S(1)} %get-tuple-element.26), kind=kCustom, calls=%fused_computation | custom fusion | bytes 1967616 | tf_op jit(solution)/shard_map/gather | solution.py:47
  15.5 6.3 %all-to-all-start = ((bf16[8,48,1280]{2,1,0:T(8,128)(2,1)}), bf16[8,48,1280]{2,1,0:T(8,128)(2,1)S(1)}, u32[]{:S(2)}, u32[]{:S(2)}) async-start(bf16[8,48,1280]{2,1,0:T(8,128)(2,1)} %bitcast.4), calls=%async_computation | async-start | bytes 1966080 | tf_op jit(solution)/shard_map/all_to_all | solution.py:53
  21.8 1.0 concatenate.10
  22.8 2.8 %gather_fusion.1 = bf16[384,1280]{1,0:T(8,128)(2,1)} fusion(bf16[129,1280]{1,0:T(8,128)(2,1)S(1)} %concatenate.10, s32[1024]{0:T(1024)S(1)} %get-tuple-element.26), kind=kCustom, calls=%fused_computation.1 | custom fusion | bytes 1967616 | tf_op jit(solution)/shard_map/gather | solution.py:48
  25.6 21.4 %all-to-all-done = bf16[8,48,1280]{2,1,0:T(8,128)(2,1)S(1)} async-done(((bf16[8,48,1280]{2,1,0:T(8,128)(2,1)}), bf16[8,48,1280]{2,1,0:T(8,128)(2,1)S(1)}, u32[]{:S(2)}, u32[]{:S(2)}) %all-to-all-start) | async-done | bytes 983072 | tf_op jit(solution)/shard_map/all_to_all | solution.py:53
  47.0 0.9 copy-done.3
  48.0 3.6 %all-to-all-start.1 = ((bf16[8,48,1280]{2,1,0:T(8,128)(2,1)}), bf16[8,48,1280]{2,1,0:T(8,128)(2,1)S(1)}, u32[]{:S(2)}, u32[]{:S(2)}) async-start(bf16[8,48,1280]{2,1,0:T(8,128)(2,1)} %bitcast.107), calls=%async_computation.1 | async-start | bytes 1966080 | tf_op jit(solution)/shard_map/all_to_all | solution.py:60
  51.5 0.0 reduce-scatter.4.cloned.1.call-start
  51.6 0.0 copy-start.4
  51.6 2.9 %fusion.25 = bf16[384,1,768]{2,0,1:T(8,128)(2,1)S(1)} fusion(bf16[384,1280]{1,0:T(8,128)(2,1)} %bitcast.109, bf16[1,1280,768]{2,1,0:T(8,128)(2,1)} %param.12), kind=kOutput, calls=%fused_computation.29 | convolution fusion | flops 755269632 | bytes 3538944 | tf_op jit(solution)/shard_map/dot_general | solution.py:80
  54.5 1.7 fusion.28
  56.2 20.4 %all-to-all-done.1 = bf16[8,48,1280]{2,1,0:T(8,128)(2,1)S(1)} async-done(((bf16[8,48,1280]{2,1,0:T(8,128)(2,1)}), bf16[8,48,1280]{2,1,0:T(8,128)(2,1)S(1)}, u32[]{:S(2)}, u32[]{:S(2)}) %all-to-all-start.1) | async-done | bytes 983072 | tf_op jit(solution)/shard_map/all_to_all | solution.py:60
  76.6 2.9 %fusion.22 = bf16[384,1,768]{2,0,1:T(8,128)(2,1)S(1)} fusion(bf16[384,1280]{1,0:T(8,128)(2,1)S(1)} %bitcast.106, bf16[1,768,1280]{2,1,0:T(8,128)(2,1)} %param.13), kind=kOutput, calls=%fused_computation.28 | convolution fusion | flops 755269632 | bytes 3538944 | tf_op jit(solution)/shard_map/dot_general | solution.py:8
  79.5 1.4 pad_maximum_fusion
  81.0 5.2 %copy.32 = bf16[384,3,768]{0,1,2:T(4,128)(2,1)} copy(bf16[384,3,768]{2,0,1:T(8,128)(2,1)} %pad_maximum_fusion) | data formatting | bytes 3538944
  86.2 3.2 %copy.34 = bf16[96,8,3,384]{3,1,2,0:T(8,128)(2,1)} copy(bf16[96,8,3,384]{3,2,1,0:T(4,128)(2,1)} %bitcast.104) | data formatting | bytes 3538944
  89.3 0.0 reduce-scatter.4.cloned.1.call-update
  89.4 0.0 all-gather.2.cloned.1.call-start
  89.4 0.1 copy.27
  89.6 0.1 reshape.142
  89.7 2.8 %gather_fusion.2 = bf16[384]{0:T(512)(128)(2,1)S(1)} fusion(bf16[257]{0:T(512)(128)(2,1)S(1)} %pad_maximum_fusion.2, s32[1024]{0:T(1024)S(1)} %get-tuple-element.25), kind=kCustom, calls=%fused_computation.2 | custom fusion | bytes 3072 | tf_op jit(solution)/shard_map/gather | solution.py:49
  92.5 0.1 all_to_all.25
  92.6 7.9 %all_to_all.31 = bf16[8,1,48]{2,1,0:T(2,128)(2,1)S(1)} all-to-all(bf16[8,1,48]{2,1,0:T(2,128)(2,1)S(1)} %all_to_all.25), channel_id=1, replica_groups=mesh['expert'=4,'dp'=8] {'dp'}, dimensions={0} | all-to-all | bytes 1536 | tf_op jit(solution)/shard_map/all_to_all | solution.py:67
  100.6 0.1 reshape.147
  100.6 20.2 %reduce-scatter.4.cloned.1.call-done = bf16[192,1152]{1,0:T(8,128)(2,1)} async-done(((bf16[768,1152]{1,0:T(8,128)(2,1)}), bf16[192,1152]{1,0:T(8,128)(2,1)}) %reduce-scatter.4.cloned.1.call-update) | async-done | bytes 442384
  120.9 1.4 reshape.204
  122.3 1.3 copy.33
  123.6 1.2 convert_element_type.95
  124.8 0.2 multiply_convert_fusion.2
  125.0 1.0 pad_maximum_fusion.1
  126.0 2.1 copy.29
  128.0 0.0 all-gather.2.cloned.1.call-update
  128.1 0.2 fusion.31
  128.3 0.7 convert_element_type.121
  129.0 4.6 %all-to-all-start.4 = ((bf16[8,1,48]{2,1,0:T(2,128)(2,1)}), bf16[8,1,48]{2,1,0:T(2,128)(2,1)S(1)}, u32[]{:S(2)}, u32[]{:S(2)}) async-start(bf16[8,1,48]{2,1,0:T(2,128)(2,1)} %convert_element_type.121), calls=%async_computation.4 | async-start | bytes 8192 | tf_op jit(solution)/shard_map/all_to_all | solution.py:111
  133.6 27.2 %all-gather.2.cloned.1.call-done = bf16[384,3,768]{0,2,1:T(8,128)(2,1)} async-done(((bf16[384,3,192]{0,2,1:T(8,128)(2,1)}), bf16[384,3,768]{0,2,1:T(8,128)(2,1)}) %all-gather.2.cloned.1.call-update) | async-done | bytes 1769488 | tf_op jit(solution)/shard_map/all_gather | solution.py:92
  160.8 2.2 %fusion.9 = f32[384,1280]{1,0:T(8,128)S(1)} fusion(bf16[1,1280,768]{2,1,0:T(8,128)(2,1)S(1)} %copy-done, bf16[384,3,768]{0,2,1:T(8,128)(2,1)} %all-gather.2.cloned.1.call-done), kind=kOutput, calls=%fused_computation.19 | convolution fusion | flops 754974720 | bytes 4521984 | tf_op jit(solution)/shard_map/dot_general | solution.py:8
  163.0 3.1 %fusion.3 = bf16[384,1280]{1,0:T(8,128)(2,1)} fusion(f32[384,1280]{1,0:T(8,128)S(1)} %fusion.9, bf16[1,1280,768]{2,1,0:T(8,128)(2,1)S(1)} %copy-done.9, bf16[384,3,768]{0,2,1:T(8,128)(2,1)} %all-gather.2.cloned.1.call-done), kind=kOutput, calls=%fused_computation.13 | convolution fusion | flops 755957760 | bytes 5505024 | tf_op jit(solution)/shard_map/dot_general | solution.py:8
  166.1 4.7 %all-to-all-start.3 = ((bf16[8,48,1280]{2,1,0:T(8,128)(2,1)}), bf16[8,48,1280]{2,1,0:T(8,128)(2,1)}, u32[]{:S(2)}, u32[]{:S(2)}) async-start(bf16[8,48,1280]{2,1,0:T(8,128)(2,1)} %bitcast.113), calls=%async_computation.3 | async-start | bytes 1966080 | tf_op jit(solution)/shard_map/all_to_all | solution.py:104
  170.9 1.2 multiply_convert_fusion
  172.0 0.1 reshape.150
  172.1 1.9 gather_fusion.4
  174.1 0.1 reshape.146
  174.2 16.2 %psum.7 = f32[128,2]{1,0:T(8,128)S(1)} all-reduce(f32[128,2]{1,0:T(8,128)S(1)} %reshape.146), channel_id=1, replica_groups=mesh['expert'=4,'dp'=8] {'expert'}, use_global_device_ids=true, to_apply=%region_7.8 | all-reduce | flops 256 | bytes 2048 | tf_op jit(solution)/shard_map/psum | solution.py:124
  190.4 0.6 copy.31
  191.0 4.0 %fusion = bf16[1,1280,768]{2,1,0:T(8,128)(2,1)} fusion(bf16[384,1280]{1,0:T(8,128)(2,1)} %bitcast.110, bf16[384,3,768]{0,2,1:T(8,128)(2,1)} %all-gather.2.cloned.1.call-done), kind=kOutput, calls=%fused_computation.10 | convolution fusion | flops 755957760 | bytes 3538944 | tf_op jit(solution)/shard_map/dot_general | solution.py:14
  195.0 2.5 %fusion.1 = bf16[1,1280,768]{2,1,0:T(8,128)(2,1)} fusion(bf16[384,1280]{1,0:T(8,128)(2,1)S(1)} %bitcast.112, bf16[384,3,768]{0,2,1:T(8,128)(2,1)S(1)} %copy-done.10), kind=kOutput, calls=%fused_computation.11 | convolution fusion | flops 755957760 | bytes 3538944 | tf_op jit(solution)/shard_map/dot_general | solution.py:14
  197.6 2.4 %fusion.2 = bf16[1,768,1280]{2,1,0:T(8,128)(2,1)} fusion(bf16[384,1280]{1,0:T(8,128)(2,1)S(1)} %bitcast.114, bf16[384,3,768]{0,2,1:T(8,128)(2,1)S(1)} %copy-done.10), kind=kOutput, calls=%fused_computation.12 | convolution fusion | flops 755957760 | bytes 3538944 | tf_op jit(solution)/shard_map/dot_general | solution.py:14
  200.0 2.6 %bitcast_convert_fusion = f32[384,1280]{1,0:T(8,128)} fusion(bf16[8,48,1280]{2,1,0:T(8,128)(2,1)} %all-to-all-done.3), kind=kLoop, calls=%fused_computation.31 | loop fusion | flops 491520 | bytes 2949120 | tf_op jit(solution)/shard_map/reshape | solution.py:119
  202.6 3.3 %gather_fusion.3 = f32[256,1280]{1,0:T(8,128)S(1)} fusion(f32[384,1280]{1,0:T(8,128)} %bitcast_convert_fusion, s32[1024]{0:T(1024)S(1)} %pad_clamp_fusion), kind=kCustom, calls=%fused_computation.3 | custom fusion | bytes 2622464 | tf_op jit(solution)/shard_map/gather | solution.py:119
  206.0 1.8 reshape.145
  207.8 3.6 %reduce_sum.31 = bf16[128,1280]{1,0:T(8,128)(2,1)} reduce(f32[128,2,1280]{2,1,0:T(2,128)} %reshape.145, f32[]{:T(128)} %constant.40.clone.1), dimensions={1}, to_apply=%region_5.6 | reduce | flops 163840 | bytes 1638404 | tf_op jit(solution)/shard_map/reduce_sum | solution.py:122
  (33 shorter events, 0.2 us)
Async XLA Ops:
  7.2 47.3 %copy-start = (bf16[1,1280,768]{2,1,0:T(8,128)(2,1)S(1)}, bf16[1,1280,768]{2,1,0:T(8,128)(2,1)}, u32[]{:S(2)}) copy-start(bf16[1,1280,768]{2,1,0:T(8,128)(2,1)} %param.11) | copy-start | bytes 5898244
  15.5 31.5 %all-to-all-start = ((bf16[8,48,1280]{2,1,0:T(8,128)(2,1)}), bf16[8,48,1280]{2,1,0:T(8,128)(2,1)S(1)}, u32[]{:S(2)}, u32[]{:S(2)}) async-start(bf16[8,48,1280]{2,1,0:T(8,128)(2,1)} %bitcast.4), calls=%async_computation | async-start | bytes 1966080 | tf_op jit(solution)/shard_map/all_to_all | solution.py:53
  47.0 0.9 copy-start.3
  48.0 28.7 %all-to-all-start.1 = ((bf16[8,48,1280]{2,1,0:T(8,128)(2,1)}), bf16[8,48,1280]{2,1,0:T(8,128)(2,1)S(1)}, u32[]{:S(2)}, u32[]{:S(2)}) async-start(bf16[8,48,1280]{2,1,0:T(8,128)(2,1)} %bitcast.107), calls=%async_computation.1 | async-start | bytes 1966080 | tf_op jit(solution)/shard_map/all_to_all | solution.py:60
  51.5 69.4 %reduce-scatter.4.cloned.1.call-start = ((), (), s32[]{:S(2)}) async-start(), calls=%async_computation.7 | async-start | bytes 2211840
  51.6 2.9 %copy-start.4 = (bf16[8,48,1280]{2,1,0:T(8,128)(2,1)S(1)}, bf16[8,48,1280]{2,1,0:T(8,128)(2,1)}, u32[]{:S(2)}) copy-start(bf16[8,48,1280]{2,1,0:T(8,128)(2,1)} %copy-done.3) | copy-start | bytes 2949124
  76.6 2.9 %copy-start.1 = (bf16[8,48,1280]{2,1,0:T(8,128)(2,1)}, bf16[8,48,1280]{2,1,0:T(8,128)(2,1)S(1)}, u32[]{:S(2)}) copy-start(bf16[8,48,1280]{2,1,0:T(8,128)(2,1)S(1)} %all-to-all-done.1) | copy-start | bytes 2949124
  76.6 2.9 %copy-start.7 = (bf16[384,1,768]{2,0,1:T(8,128)(2,1)S(1)}, bf16[384,1,768]{2,0,1:T(8,128)(2,1)}, u32[]{:S(2)}) copy-start(bf16[384,1,768]{2,0,1:T(8,128)(2,1)} %fusion.28) | copy-start | bytes 1769476
  86.1 3.3 %copy-start.8 = (bf16[128,2]{0,1:T(2,128)(2,1)S(1)}, bf16[128,2]{0,1:T(2,128)(2,1)}, u32[]{:S(2)}) copy-start(bf16[128,2]{0,1:T(2,128)(2,1)} %param.9) | copy-start | bytes 1540
  89.4 71.4 %all-gather.2.cloned.1.call-start = ((), (), s32[]{:S(2)}) async-start(), calls=%async_computation.6 | async-start | bytes 2211840 | tf_op jit(solution)/shard_map/all_gather | solution.py:92
  129.0 37.1 %all-to-all-start.4 = ((bf16[8,1,48]{2,1,0:T(2,128)(2,1)}), bf16[8,1,48]{2,1,0:T(2,128)(2,1)S(1)}, u32[]{:S(2)}, u32[]{:S(2)}) async-start(bf16[8,1,48]{2,1,0:T(2,128)(2,1)} %convert_element_type.121), calls=%async_computation.4 | async-start | bytes 8192 | tf_op jit(solution)/shard_map/all_to_all | solution.py:111
  160.8 2.2 %copy-start.9 = (bf16[1,1280,768]{2,1,0:T(8,128)(2,1)S(1)}, bf16[1,1280,768]{2,1,0:T(8,128)(2,1)}, u32[]{:S(2)}) copy-start(bf16[1,1280,768]{2,1,0:T(8,128)(2,1)} %param.12) | copy-start | bytes 5898244
  166.1 4.8 %copy-start.2 = (bf16[8,48,1280]{2,1,0:T(8,128)(2,1)S(1)}, bf16[8,48,1280]{2,1,0:T(8,128)(2,1)}, u32[]{:S(2)}) copy-start(bf16[8,48,1280]{2,1,0:T(8,128)(2,1)} %copy-done.1) | copy-start | bytes 2949124
  166.1 33.9 %all-to-all-start.3 = ((bf16[8,48,1280]{2,1,0:T(8,128)(2,1)}), bf16[8,48,1280]{2,1,0:T(8,128)(2,1)}, u32[]{:S(2)}, u32[]{:S(2)}) async-start(bf16[8,48,1280]{2,1,0:T(8,128)(2,1)} %bitcast.113), calls=%async_computation.3 | async-start | bytes 1966080 | tf_op jit(solution)/shard_map/all_to_all | solution.py:104
  174.2 20.8 %copy-start.5 = (bf16[8,48,1280]{2,1,0:T(8,128)(2,1)S(1)}, bf16[8,48,1280]{2,1,0:T(8,128)(2,1)}, u32[]{:S(2)}) copy-start(bf16[8,48,1280]{2,1,0:T(8,128)(2,1)} %copy-done.3) | copy-start | bytes 2949124
  191.0 4.0 %copy-start.10 = (bf16[384,3,768]{0,2,1:T(8,128)(2,1)S(1)}, bf16[384,3,768]{0,2,1:T(8,128)(2,1)}, u32[]{:S(2)}) copy-start(bf16[384,3,768]{0,2,1:T(8,128)(2,1)} %all-gather.2.cloned.1.call-done) | copy-start | bytes 5308420
  195.0 2.5 %copy-start.6 = (bf16[8,48,1280]{2,1,0:T(8,128)(2,1)S(1)}, bf16[8,48,1280]{2,1,0:T(8,128)(2,1)}, u32[]{:S(2)}) copy-start(bf16[8,48,1280]{2,1,0:T(8,128)(2,1)} %multiply_convert_fusion) | copy-start | bytes 2949124
Sparse Core Ops, SparseCore 0:
  89.5 31.3 reduce-scatter.3
  128.2 32.5 all-gather.1
where the time goes:
time: 219 us; the launch traced here: 218 us
  waiting for transfers between devices  89.4 us (41%)
  local copies, waits for them, and re-layouts  36.5 us (17%)
  blocking collectives  24.1 us (11%)
  matrix products  21.7 us (10%)
  starting transfers between devices  19.3 us (9%)
  between operations  14.3 us (7%)
  other arithmetic  13 us (6%)
    all_gather x1, waiting for transfers between devices, body(): lax.all_gather(jnp.stack([hidden_part, gate_part, up_part], axis=1), 'exp...  27.2 us
    all_to_all x1, waiting for transfers between devices, body(): lax.all_to_all(token_send.reshape(experts, capacity, slice_width), 'dp',...  21.4 us
    all_to_all x1, waiting for transfers between devices, body(): lax.all_to_all(cot_send.reshape(experts, capacity, slice_width), 'dp', sp...  20.4 us
    unnamed x3, waiting for transfers between devices  20.3 us
    psum x1, blocking collectives, body(): combine_grad = lax.psum(comb_part, 'expert')  16.2 us
    unnamed x29, local copies, waits for them, and re-layouts  13.6 us
    dot_general x3, matrix products, contract_first(): lax.dot_general(matrix_a, matrix_b, (((0,), (0,)), ((), ())), preferred_e...  8.94 us
    dot_general x3, matrix products, contract_last(): lax.dot_general(matrix_a, matrix_b, (((1,), (1,)), ((), ())), preferred_e...  8.15 us
  transfers between devices with their start and end apart: 6, of which 4 were waited for; matrix products, arithmetic and copies ran while one was open for 14% of the time, Pallas kernels for 0%

commit v1 on v0

--- a/solution.py
+++ b/solution.py
@@ -2,6 +2,14 @@
 import jax.numpy as jnp
 from jax import lax
 from jax.sharding import PartitionSpec as P
+
+
+def add_in_pairs(shard, mesh_axis):
+    size, summed = (lax.axis_size(mesh_axis), shard)
+    for far in [1 << k for k in range(size.bit_length() - 1)]:
+        swap = [(i, i ^ far) for i in range(size)]
+        summed = summed + lax.ppermute(summed, mesh_axis, swap)
+    return summed
 
 
 def contract_last(matrix_a, matrix_b):
@@ -121,7 +129,7 @@
     )
     token_grad = jnp.sum(route_dx, axis=1).astype(jnp.bfloat16)
     comb_part = back_comb.reshape(slot_total)[places].reshape(tok_rows, top_routes)
-    combine_grad = lax.psum(comb_part, "expert")
+    combine_grad = add_in_pairs(comb_part, "expert")
     return (token_grad, combine_grad, grad_gate, grad_up, grad_down)
 
 

time: 219 us -> 215 us (0.982)
  blocking collectives: 24.1 us -> 7.92 us
  waiting for transfers between devices: 89.4 us -> 98.6 us
  starting transfers between devices: 19.3 us -> 22.4 us
    psum x1 -> x0, blocking collectives: 16.2 us -> none  [body(): combine_grad = lax.psum(comb_part, 'expert')]
    ppermute x0 -> x2, waiting for transfers between devices: none -> 4.66 us  [add_in_pairs(): summed = summed + lax.ppermute(summed, mesh_axis, swap)]
    all_to_all x1, waiting for transfers between devices: 0.01 us -> 4.57 us  [body(): lax.all_to_all(slot_dx.reshape(experts, capacity, slice_width).astype(jnp...]
    ppermute x0 -> x2, starting transfers between devices: none -> 3.06 us  [add_in_pairs(): summed = summed + lax.ppermute(summed, mesh_axis, swap)]
  transfers between devices with their start and end apart: 6 -> 8, of which waited for: 4 -> 7; matrix products, arithmetic and copies ran while one was open for 14% -> 14% of each run, Pallas kernels for 0% -> 0%
where the time goes in v1:
time: 215 us; the launch traced here: 214 us
  waiting for transfers between devices  98.6 us (46%)
  local copies, waits for them, and re-layouts  36.6 us (17%)
  starting transfers between devices  22.4 us (10%)
  matrix products  21.7 us (10%)
  between operations  14.3 us (7%)
  other arithmetic  12.9 us (6%)
  blocking collectives  7.92 us (4%)
    all_gather x1, waiting for transfers between devices, body(): lax.all_gather(jnp.stack([hidden_part, gate_part, up_part], axis=1), 'exp...  27.2 us
    all_to_all x1, waiting for transfers between devices, body(): lax.all_to_all(token_send.reshape(experts, capacity, slice_width), 'dp',...  21.4 us
    all_to_all x1, waiting for transfers between devices, body(): lax.all_to_all(cot_send.reshape(experts, capacity, slice_width), 'dp', sp...  20.4 us
    unnamed x3, waiting for transfers between devices  20.3 us
    unnamed x29, local copies, waits for them, and re-layouts  13.8 us
    dot_general x3, matrix products, contract_first(): lax.dot_general(matrix_a, matrix_b, (((0,), (0,)), ((), ())), preferred_e...  8.94 us
    dot_general x3, matrix products, contract_last(): lax.dot_general(matrix_a, matrix_b, (((1,), (1,)), ((), ())), preferred_e...  8.15 us
    all_to_all x1, blocking collectives, body(): lax.all_to_all(comb_send.reshape(experts, capacity), 'dp', split_axis=0,...  7.92 us
  transfers between devices with their start and end apart: 8, of which 7 were waited for; matrix products, arithmetic and copies ran while one was open for 14% of the time, Pallas kernels for 0%

profile of v1, /device:TPU:0, one launch (start us, length us, event | category | flops | bytes accessed | tf_op | source)
XLA Modules:
  0.0 214.4 jit_solution(7763856593935259037)
XLA Ops:
  7.2 0.9 copy.25
  8.1 0.1 eq.29
  8.2 0.1 eq.25
  8.4 0.7 broadcast_multiply_fusion
  9.1 0.6 reduce-window.6
  9.6 0.2 slice_reduce_fusion
  9.9 0.1 copy.24
  10.0 0.1 mul.76
  10.2 0.1 fusion.38
  10.3 1.4 scatter_custom_fusion
  11.7 1.0 concatenate.9
  12.7 2.8 %gather_fusion = bf16[384,1280]{1,0:T(8,128)(2,1)} fusion(bf16[129,1280]{1,0:T(8,128)(2,1)S(1)} %concatenate.9, s32[1024]{0:T(1024)S(1)} %get-tuple-element.26), kind=kCustom, calls=%fused_computation | custom fusion | bytes 1967616 | tf_op jit(solution)/shard_map/gather | solution.py:55
  15.5 6.3 %all-to-all-start = ((bf16[8,48,1280]{2,1,0:T(8,128)(2,1)}), bf16[8,48,1280]{2,1,0:T(8,128)(2,1)S(1)}, u32[]{:S(2)}, u32[]{:S(2)}) async-start(bf16[8,48,1280]{2,1,0:T(8,128)(2,1)} %bitcast.4), calls=%async_computation | async-start | bytes 1966080 | tf_op jit(solution)/shard_map/all_to_all | solution.py:61
  21.8 1.0 concatenate.10
  22.8 2.8 %gather_fusion.1 = bf16[384,1280]{1,0:T(8,128)(2,1)} fusion(bf16[129,1280]{1,0:T(8,128)(2,1)S(1)} %concatenate.10, s32[1024]{0:T(1024)S(1)} %get-tuple-element.26), kind=kCustom, calls=%fused_computation.1 | custom fusion | bytes 1967616 | tf_op jit(solution)/shard_map/gather | solution.py:56
  25.6 21.4 %all-to-all-done = bf16[8,48,1280]{2,1,0:T(8,128)(2,1)S(1)} async-done(((bf16[8,48,1280]{2,1,0:T(8,128)(2,1)}), bf16[8,48,1280]{2,1,0:T(8,128)(2,1)S(1)}, u32[]{:S(2)}, u32[]{:S(2)}) %all-to-all-start) | async-done | bytes 983072 | tf_op jit(solution)/shard_map/all_to_all | solution.py:61
  47.0 0.9 copy-done.3
  47.9 3.6 %all-to-all-start.1 = ((bf16[8,48,1280]{2,1,0:T(8,128)(2,1)}), bf16[8,48,1280]{2,1,0:T(8,128)(2,1)S(1)}, u32[]{:S(2)}, u32[]{:S(2)}) async-start(bf16[8,48,1280]{2,1,0:T(8,128)(2,1)} %bitcast.107), calls=%async_computation.1 | async-start | bytes 1966080 | tf_op jit(solution)/shard_map/all_to_all | solution.py:68
  51.5 0.0 reduce-scatter.4.cloned.1.call-start
  51.6 2.9 %fusion.25 = bf16[384,1,768]{2,0,1:T(8,128)(2,1)S(1)} fusion(bf16[384,1280]{1,0:T(8,128)(2,1)} %bitcast.109, bf16[1,1280,768]{2,1,0:T(8,128)(2,1)} %param.12), kind=kOutput, calls=%fused_computation.29 | convolution fusion | flops 755269632 | bytes 3538944 | tf_op jit(solution)/shard_map/dot_general | solution.py:88
  54.4 1.7 fusion.28
  56.2 20.4 %all-to-all-done.1 = bf16[8,48,1280]{2,1,0:T(8,128)(2,1)S(1)} async-done(((bf16[8,48,1280]{2,1,0:T(8,128)(2,1)}), bf16[8,48,1280]{2,1,0:T(8,128)(2,1)S(1)}, u32[]{:S(2)}, u32[]{:S(2)}) %all-to-all-start.1) | async-done | bytes 983072 | tf_op jit(solution)/shard_map/all_to_all | solution.py:68
  76.6 2.9 %fusion.22 = bf16[384,1,768]{2,0,1:T(8,128)(2,1)S(1)} fusion(bf16[384,1280]{1,0:T(8,128)(2,1)S(1)} %bitcast.106, bf16[1,768,1280]{2,1,0:T(8,128)(2,1)} %param.13), kind=kOutput, calls=%fused_computation.28 | convolution fusion | flops 755269632 | bytes 3538944 | tf_op jit(solution)/shard_map/dot_general | solution.py:16
  79.5 1.4 pad_maximum_fusion
  80.9 5.2 %copy.32 = bf16[384,3,768]{0,1,2:T(4,128)(2,1)} copy(bf16[384,3,768]{2,0,1:T(8,128)(2,1)} %pad_maximum_fusion) | data formatting | bytes 3538944
  86.1 3.2 %copy.34 = bf16[96,8,3,384]{3,1,2,0:T(8,128)(2,1)} copy(bf16[96,8,3,384]{3,2,1,0:T(4,128)(2,1)} %bitcast.104) | data formatting | bytes 3538944
  89.3 0.0 all-gather.2.cloned.1.call-start
  89.4 0.1 copy.27
  89.5 0.1 reshape.142
  89.7 2.8 %gather_fusion.2 = bf16[384]{0:T(512)(128)(2,1)S(1)} fusion(bf16[257]{0:T(512)(128)(2,1)S(1)} %pad_maximum_fusion.2, s32[1024]{0:T(1024)S(1)} %get-tuple-element.25), kind=kCustom, calls=%fused_computation.2 | custom fusion | bytes 3072 | tf_op jit(solution)/shard_map/gather | solution.py:57
  92.5 0.1 all_to_all.25
  92.6 7.9 %all_to_all.31 = bf16[8,1,48]{2,1,0:T(2,128)(2,1)S(1)} all-to-all(bf16[8,1,48]{2,1,0:T(2,128)(2,1)S(1)} %all_to_all.25), channel_id=1, replica_groups=mesh['expert'=4,'dp'=8] {'dp'}, dimensions={0} | all-to-all | bytes 1536 | tf_op jit(solution)/shard_map/all_to_all | solution.py:75
  100.5 0.1 reshape.147
  100.6 20.2 %reduce-scatter.4.cloned.1.call-done = bf16[192,1152]{1,0:T(8,128)(2,1)} async-done(((bf16[768,1152]{1,0:T(8,128)(2,1)}), bf16[192,1152]{1,0:T(8,128)(2,1)}) %reduce-scatter.4.cloned.1.call-update) | async-done | bytes 442384
  120.9 1.4 reshape.204
  122.3 1.3 copy.33
  123.6 1.2 convert_element_type.95
  124.7 0.2 multiply_convert_fusion.2
  125.0 1.0 pad_maximum_fusion.1
  125.9 2.1 copy.29
  128.0 0.2 fusion.31
  128.3 0.7 convert_element_type.121
  128.9 4.6 %all-to-all-start.4 = ((bf16[8,1,48]{2,1,0:T(2,128)(2,1)}), bf16[8,1,48]{2,1,0:T(2,128)(2,1)S(1)}, u32[]{:S(2)}, u32[]{:S(2)}) async-start(bf16[8,1,48]{2,1,0:T(2,128)(2,1)} %convert_element_type.121), calls=%async_computation.4 | async-start | bytes 8192 | tf_op jit(solution)/shard_map/all_to_all | solution.py:119
  133.5 27.2 %all-gather.2.cloned.1.call-done = bf16[384,3,768]{0,2,1:T(8,128)(2,1)} async-done(((bf16[384,3,192]{0,2,1:T(8,128)(2,1)}), bf16[384,3,768]{0,2,1:T(8,128)(2,1)}) %all-gather.2.cloned.1.call-update) | async-done | bytes 1769488 | tf_op jit(solution)/shard_map/all_gather | solution.py:100
  160.8 2.2 %fusion.9 = f32[384,1280]{1,0:T(8,128)S(1)} fusion(bf16[1,1280,768]{2,1,0:T(8,128)(2,1)S(1)} %copy-done, bf16[384,3,768]{0,2,1:T(8,128)(2,1)} %all-gather.2.cloned.1.call-done), kind=kOutput, calls=%fused_computation.19 | convolution fusion | flops 754974720 | bytes 4521984 | tf_op jit(solution)/shard_map/dot_general | solution.py:16
  163.0 3.1 %fusion.3 = bf16[384,1280]{1,0:T(8,128)(2,1)} fusion(f32[384,1280]{1,0:T(8,128)S(1)} %fusion.9, bf16[1,1280,768]{2,1,0:T(8,128)(2,1)S(1)} %copy-done.9, bf16[384,3,768]{0,2,1:T(8,128)(2,1)} %all-gather.2.cloned.1.call-done), kind=kOutput, calls=%fused_computation.13 | convolution fusion | flops 755957760 | bytes 5505024 | tf_op jit(solution)/shard_map/dot_general | solution.py:16
  166.1 4.7 %all-to-all-start.3 = ((bf16[8,48,1280]{2,1,0:T(8,128)(2,1)}), bf16[8,48,1280]{2,1,0:T(8,128)(2,1)}, u32[]{:S(2)}, u32[]{:S(2)}) async-start(bf16[8,48,1280]{2,1,0:T(8,128)(2,1)} %bitcast.113), calls=%async_computation.3 | async-start | bytes 1966080 | tf_op jit(solution)/shard_map/all_to_all | solution.py:112
  170.8 0.1 reshape.150
  170.9 1.9 gather_fusion.4
  172.9 0.1 reshape.146
  173.0 1.5 collective-permute-start
  174.5 3.0 %collective-permute-done = f32[128,2]{1,0:T(8,128)S(1)} collective-permute-done((f32[128,2]{1,0:T(8,128)S(1)}, f32[128,2]{1,0:T(8,128)S(1)}, u32[]{:S(2)}, u32[]{:S(2)}) %collective-permute-start) | collective-permute-done | bytes 1056 | tf_op jit(solution)/shard_map/ppermute | solution.py:11
  177.6 1.5 collective-permute-start.1
  179.1 1.2 multiply_convert_fusion
  180.3 1.6 collective-permute-done.1
  181.9 0.6 copy.31
  182.6 4.0 %fusion = bf16[1,1280,768]{2,1,0:T(8,128)(2,1)} fusion(bf16[384,1280]{1,0:T(8,128)(2,1)} %bitcast.110, bf16[384,3,768]{0,2,1:T(8,128)(2,1)} %all-gather.2.cloned.1.call-done), kind=kOutput, calls=%fused_computation.10 | convolution fusion | flops 755957760 | bytes 3538944 | tf_op jit(solution)/shard_map/dot_general | solution.py:22
  186.6 2.5 %fusion.1 = bf16[1,1280,768]{2,1,0:T(8,128)(2,1)} fusion(bf16[384,1280]{1,0:T(8,128)(2,1)S(1)} %bitcast.112, bf16[384,3,768]{0,2,1:T(8,128)(2,1)S(1)} %copy-done.10), kind=kOutput, calls=%fused_computation.11 | convolution fusion | flops 755957760 | bytes 3538944 | tf_op jit(solution)/shard_map/dot_general | solution.py:22
  189.1 2.4 %fusion.2 = bf16[1,768,1280]{2,1,0:T(8,128)(2,1)} fusion(bf16[384,1280]{1,0:T(8,128)(2,1)S(1)} %bitcast.114, bf16[384,3,768]{0,2,1:T(8,128)(2,1)S(1)} %copy-done.10), kind=kOutput, calls=%fused_computation.12 | convolution fusion | flops 755957760 | bytes 3538944 | tf_op jit(solution)/shard_map/dot_general | solution.py:22
  191.5 4.6 %all-to-all-done.3 = bf16[8,48,1280]{2,1,0:T(8,128)(2,1)} async-done(((bf16[8,48,1280]{2,1,0:T(8,128)(2,1)}), bf16[8,48,1280]{2,1,0:T(8,128)(2,1)}, u32[]{:S(2)}, u32[]{:S(2)}) %all-to-all-start.3) | async-done | bytes 983072 | tf_op jit(solution)/shard_map/all_to_all | solution.py:112
  196.1 2.6 %bitcast_convert_fusion = f32[384,1280]{1,0:T(8,128)} fusion(bf16[8,48,1280]{2,1,0:T(8,128)(2,1)} %all-to-all-done.3), kind=kLoop, calls=%fused_computation.31 | loop fusion | flops 491520 | bytes 2949120 | tf_op jit(solution)/shard_map/reshape | solution.py:127
  198.7 3.3 %gather_fusion.3 = f32[256,1280]{1,0:T(8,128)S(1)} fusion(f32[384,1280]{1,0:T(8,128)} %bitcast_convert_fusion, s32[1024]{0:T(1024)S(1)} %pad_clamp_fusion), kind=kCustom, calls=%fused_computation.3 | custom fusion | bytes 2622464 | tf_op jit(solution)/shard_map/gather | solution.py:127
  202.1 1.8 reshape.145
  203.9 3.6 %reduce_sum.31 = bf16[128,1280]{1,0:T(8,128)(2,1)} reduce(f32[128,2,1280]{2,1,0:T(2,128)} %reshape.145, f32[]{:T(128)} %constant.40.clone.1), dimensions={1}, to_apply=%region_5.6 | reduce | flops 163840 | bytes 1638404 | tf_op jit(solution)/shard_map/reduce_sum | solution.py:130
  (38 shorter events, 0.2 us)
Async XLA Ops:
  7.2 47.3 %copy-start = (bf16[1,1280,768]{2,1,0:T(8,128)(2,1)S(1)}, bf16[1,1280,768]{2,1,0:T(8,128)(2,1)}, u32[]{:S(2)}) copy-start(bf16[1,1280,768]{2,1,0:T(8,128)(2,1)} %param.11) | copy-start | bytes 5898244
  15.5 31.5 %all-to-all-start = ((bf16[8,48,1280]{2,1,0:T(8,128)(2,1)}), bf16[8,48,1280]{2,1,0:T(8,128)(2,1)S(1)}, u32[]{:S(2)}, u32[]{:S(2)}) async-start(bf16[8,48,1280]{2,1,0:T(8,128)(2,1)} %bitcast.4), calls=%async_computation | async-start | bytes 1966080 | tf_op jit(solution)/shard_map/all_to_all | solution.py:61
  47.0 0.9 copy-start.3
  47.9 28.7 %all-to-all-start.1 = ((bf16[8,48,1280]{2,1,0:T(8,128)(2,1)}), bf16[8,48,1280]{2,1,0:T(8,128)(2,1)S(1)}, u32[]{:S(2)}, u32[]{:S(2)}) async-start(bf16[8,48,1280]{2,1,0:T(8,128)(2,1)} %bitcast.107), calls=%async_computation.1 | async-start | bytes 1966080 | tf_op jit(solution)/shard_map/all_to_all | solution.py:68
  51.5 69.4 %reduce-scatter.4.cloned.1.call-start = ((), (), s32[]{:S(2)}) async-start(), calls=%async_computation.7 | async-start | bytes 2211840
  51.5 2.9 %copy-start.4 = (bf16[8,48,1280]{2,1,0:T(8,128)(2,1)S(1)}, bf16[8,48,1280]{2,1,0:T(8,128)(2,1)}, u32[]{:S(2)}) copy-start(bf16[8,48,1280]{2,1,0:T(8,128)(2,1)} %copy-done.3) | copy-start | bytes 2949124
  76.6 2.9 %copy-start.1 = (bf16[8,48,1280]{2,1,0:T(8,128)(2,1)}, bf16[8,48,1280]{2,1,0:T(8,128)(2,1)S(1)}, u32[]{:S(2)}) copy-start(bf16[8,48,1280]{2,1,0:T(8,128)(2,1)S(1)} %all-to-all-done.1) | copy-start | bytes 2949124
  76.6 2.9 %copy-start.7 = (bf16[384,1,768]{2,0,1:T(8,128)(2,1)S(1)}, bf16[384,1,768]{2,0,1:T(8,128)(2,1)}, u32[]{:S(2)}) copy-start(bf16[384,1,768]{2,0,1:T(8,128)(2,1)} %fusion.28) | copy-start | bytes 1769476
  86.1 3.3 %copy-start.8 = (bf16[128,2]{0,1:T(2,128)(2,1)S(1)}, bf16[128,2]{0,1:T(2,128)(2,1)}, u32[]{:S(2)}) copy-start(bf16[128,2]{0,1:T(2,128)(2,1)} %param.9) | copy-start | bytes 1540
  89.3 71.4 %all-gather.2.cloned.1.call-start = ((), (), s32[]{:S(2)}) async-start(), calls=%async_computation.6 | async-start | bytes 2211840 | tf_op jit(solution)/shard_map/all_gather | solution.py:100
  128.9 37.1 %all-to-all-start.4 = ((bf16[8,1,48]{2,1,0:T(2,128)(2,1)}), bf16[8,1,48]{2,1,0:T(2,128)(2,1)S(1)}, u32[]{:S(2)}, u32[]{:S(2)}) async-start(bf16[8,1,48]{2,1,0:T(2,128)(2,1)} %convert_element_type.121), calls=%async_computation.4 | async-start | bytes 8192 | tf_op jit(solution)/shard_map/all_to_all | solution.py:119
  160.8 2.2 %copy-start.9 = (bf16[1,1280,768]{2,1,0:T(8,128)(2,1)S(1)}, bf16[1,1280,768]{2,1,0:T(8,128)(2,1)}, u32[]{:S(2)}) copy-start(bf16[1,1280,768]{2,1,0:T(8,128)(2,1)} %param.12) | copy-start | bytes 5898244
  166.1 13.1 %copy-start.2 = (bf16[8,48,1280]{2,1,0:T(8,128)(2,1)S(1)}, bf16[8,48,1280]{2,1,0:T(8,128)(2,1)}, u32[]{:S(2)}) copy-start(bf16[8,48,1280]{2,1,0:T(8,128)(2,1)} %copy-done.1) | copy-start | bytes 2949124
  166.1 30.0 %all-to-all-start.3 = ((bf16[8,48,1280]{2,1,0:T(8,128)(2,1)}), bf16[8,48,1280]{2,1,0:T(8,128)(2,1)}, u32[]{:S(2)}, u32[]{:S(2)}) async-start(bf16[8,48,1280]{2,1,0:T(8,128)(2,1)} %bitcast.113), calls=%async_computation.3 | async-start | bytes 1966080 | tf_op jit(solution)/shard_map/all_to_all | solution.py:112
  173.0 4.6 %collective-permute-start = (f32[128,2]{1,0:T(8,128)S(1)}, f32[128,2]{1,0:T(8,128)S(1)}, u32[]{:S(2)}, u32[]{:S(2)}) collective-permute-start(f32[128,2]{1,0:T(8,128)S(1)} %reshape.146), channel_id=1, source_target_pairs={{0,8},{8,0},{16,24},{24,16},{1,9},{9,1},{17,25},{25,17},{2,10},{10... | collective-permute-start | bytes 3080 | tf_op jit(solution)/shard_map/ppermute | solution.py:11
  177.6 4.3 %collective-permute-start.1 = (f32[128,2]{1,0:T(8,128)S(1)}, f32[128,2]{1,0:T(8,128)S(1)}, u32[]{:S(2)}, u32[]{:S(2)}) collective-permute-start(f32[128,2]{1,0:T(8,128)S(1)} %add.69), channel_id=1, source_target_pairs={{0,16},{8,24},{16,0},{24,8},{1,17},{9,25},{17,1},{25,9},{2,18},{10... | collective-permute-start | bytes 3080 | tf_op jit(solution)/shard_map/ppermute | solution.py:11
  180.3 6.3 %copy-start.5 = (bf16[8,48,1280]{2,1,0:T(8,128)(2,1)S(1)}, bf16[8,48,1280]{2,1,0:T(8,128)(2,1)}, u32[]{:S(2)}) copy-start(bf16[8,48,1280]{2,1,0:T(8,128)(2,1)} %copy-done.3) | copy-start | bytes 2949124
  182.6 4.0 %copy-start.10 = (bf16[384,3,768]{0,2,1:T(8,128)(2,1)S(1)}, bf16[384,3,768]{0,2,1:T(8,128)(2,1)}, u32[]{:S(2)}) copy-start(bf16[384,3,768]{0,2,1:T(8,128)(2,1)} %all-gather.2.cloned.1.call-done) | copy-start | bytes 5308420
  186.6 2.5 %copy-start.6 = (bf16[8,48,1280]{2,1,0:T(8,128)(2,1)S(1)}, bf16[8,48,1280]{2,1,0:T(8,128)(2,1)}, u32[]{:S(2)}) copy-start(bf16[8,48,1280]{2,1,0:T(8,128)(2,1)} %multiply_convert_fusion) | copy-start | bytes 2949124
Sparse Core Ops, SparseCore 0:
  89.5 31.3 reduce-scatter.3
  128.2 32.5 all-gather.1
